TPU v7x, 32 devices: a whole 2x2x4 slice. The times are simulated.
32 devices in a mesh: vis: 8 (over y, x, core), wav: 4 (over z).
Axes of the slice: x: 2, y: 2, z: 4, core: 2. Of those that a mesh axis runs over, the one named last changes fastest.
Arguments:
- image: float32 [4096, 4096], P('vis', 'wav'), may hold values from -6 to 6
- kernel_v: bfloat16 [1024, 64, 256], P(('vis', 'wav')), may hold values from -0.5 to 0.5
- kernel_u: bfloat16 [1024, 64, 256], P(('vis', 'wav')), may hold values from -0.5 to 0.5
- measured: bfloat16 [1024, 2, 256], P(('vis', 'wav')), may hold values from -4 to 4
- dest_owner: int32 [1024, 1], P(('vis', 'wav')), may hold values from 0 to 7; in each aligned block of 32 rows (0 to 31, 32 to 63, ...) at most 8 rows name the same one
- patch_slot: int32 [1024], P(('vis', 'wav')), may hold values from 0 to 127
- thresholds: float32 [4], replicated, may hold values from 0.1 to 1
Outputs:
- restored: float32 [4096, 4096], P('vis', 'wav')
- residual: float32 [1024, 2, 256], P(('vis', 'wav'))
Inputs may be any that keep to these rules, and one draw needn't show every extreme that they name: `dest_owner`: the vis index of the owner of the block's uv cells; the 32 blocks of one device name one owner at most 8 times, a bound that some block reaches. `patch_slot`: the block's kernel block among the 128 of its owner's tile in the band of the block's wav index.
All inputs are finite; a program needn't handle non-finite values.
Results may differ from a plain program's by a relative error of at most 0.0017.
Values may be sent and summed in bfloat16 or wider, within the bound.
No kernel may reach another device: no remote copies, remote signals or barrier semaphores. Data moves between devices by JAX's collectives and lax.ppermute only.
A program may use at most 128 MiB of HBM per device.

v0:
```python
import math
import jax
import jax.numpy as jnp
import numpy as np
from jax import lax
from jax.sharding import PartitionSpec as P

IMG = 4096
PATCH = 64
FA = 64
FB = 64
HIGHEST = lax.Precision.HIGHEST


def haar_table():
    rows = np.zeros((8, 8))
    root = 1.0 / np.sqrt(8.0)
    rows[0, :] = root
    rows[1, :4] = root
    rows[1, 4:] = -root
    rows[2, 0:2] = 0.5
    rows[2, 2:4] = -0.5
    rows[3, 4:6] = 0.5
    rows[3, 6:8] = -0.5
    for index in range(4):
        rows[4 + index, 2 * index] = np.sqrt(0.5)
        rows[4 + index, 2 * index + 1] = -np.sqrt(0.5)
    return np.kron(np.eye(16), rows)


def basis_prox(field, shift, limit, table):
    height, width = field.shape
    moved = jnp.roll(field, -shift, axis=1).reshape(height, width // 128, 128)
    coeff = jnp.einsum("rgj,kj->rgk", moved, table, precision=HIGHEST)
    coeff = coeff.reshape(height // 2, 2, width // 128, 128)
    factor = math.sqrt(0.5)
    upper = (coeff[:, 0] + coeff[:, 1]) * factor
    lower = (coeff[:, 0] - coeff[:, 1]) * factor
    upper = upper - jnp.clip(upper, -limit, limit)
    lower = lower - jnp.clip(lower, -limit, limit)
    coeff = jnp.stack([(upper + lower) * factor, (upper - lower) * factor], 1)
    coeff = coeff.reshape(height, width // 128, 128)
    back = jnp.einsum("rgk,kj->rgj", coeff, table, precision=HIGHEST)
    return jnp.roll(back.reshape(height, width), shift, axis=1)


def dft_tables(sign):
    first_idx = jnp.arange(FA, dtype=jnp.int32)
    second_idx = jnp.arange(FB, dtype=jnp.int32)
    first_angle = (first_idx[:, None] * first_idx[None, :] % FA).astype(jnp.float32) * (
        2.0 * math.pi / FA
    )
    twist_angle = (first_idx[:, None] * second_idx[None, :] % IMG).astype(jnp.float32) * (
        2.0 * math.pi / IMG
    )
    second_angle = (second_idx[:, None] * second_idx[None, :] % FB).astype(jnp.float32) * (
        2.0 * math.pi / FB
    )
    return (
        jnp.cos(first_angle),
        sign * jnp.sin(first_angle),
        jnp.cos(twist_angle),
        sign * jnp.sin(twist_angle),
        jnp.cos(second_angle),
        sign * jnp.sin(second_angle),
    )


def dft_last(real_part, imag_part, tables, want_imag):
    first_cos, first_sin, twist_cos, twist_sin, second_cos, second_sin = tables
    leading = real_part.shape[:-1]
    real_in = real_part.reshape(leading + (FA, FB))
    mix_real = jnp.einsum("ka,...ab->...kb", first_cos, real_in, precision=HIGHEST)
    mix_imag = jnp.einsum("ka,...ab->...kb", first_sin, real_in, precision=HIGHEST)
    if imag_part is not None:
        imag_in = imag_part.reshape(leading + (FA, FB))
        mix_real = mix_real - jnp.einsum("ka,...ab->...kb", first_sin, imag_in, precision=HIGHEST)
        mix_imag = mix_imag + jnp.einsum("ka,...ab->...kb", first_cos, imag_in, precision=HIGHEST)
    turned_real = mix_real * twist_cos - mix_imag * twist_sin
    turned_imag = mix_real * twist_sin + mix_imag * twist_cos
    factor = 1.0 / math.sqrt(IMG)
    out_real = jnp.einsum("...kb,jb->...jk", turned_real, second_cos, precision=HIGHEST)
    out_real = out_real - jnp.einsum("...kb,jb->...jk", turned_imag, second_sin, precision=HIGHEST)
    out_real = out_real.reshape(leading + (IMG,)) * factor
    if not want_imag:
        return (out_real, None)
    out_imag = jnp.einsum("...kb,jb->...jk", turned_real, second_sin, precision=HIGHEST)
    out_imag = out_imag + jnp.einsum("...kb,jb->...jk", turned_imag, second_cos, precision=HIGHEST)
    return (out_real, out_imag.reshape(leading + (IMG,)) * factor)


def degrid_values(v_side_length, u_side_length, grid_patch, measurements):
    product = jnp.einsum(
        "nac,nat->nct", grid_patch, v_side_length, preferred_element_type=jnp.float32
    )
    width = u_side_length.shape[1]
    sky_model_real = jnp.sum(product[:, :width] * u_side_length, 1)
    sky_model_imag = jnp.sum(product[:, width:] * u_side_length, 1)
    return jnp.stack([sky_model_real, sky_model_imag], 1) - measurements.astype(jnp.float32)


def grid_terms(v_side_length, u_side_length, misfit):
    weighted = jnp.concatenate(
        [misfit[:, 0, None, :] * u_side_length, misfit[:, 1, None, :] * u_side_length], 1
    ).astype(jnp.bfloat16)
    return jnp.einsum("nat,nct->nac", v_side_length, weighted, preferred_element_type=jnp.float32)


def shards(image, kernel_v, kernel_u, measured, dest_owner, patch_slot, thresholds):
    vis_count = lax.axis_size("vis")
    wav_count = lax.axis_size("wav")
    block_count = kernel_v.shape[0]
    capacity = 2 * block_count // vis_count
    slot_total = capacity * vis_count
    strip = IMG // (vis_count * wav_count)
    kv_size = IMG // vis_count
    ku_size = IMG // wav_count
    tile_down = kv_size // PATCH
    tile_across = ku_size // PATCH
    patch_count = tile_down * tile_across
    table = jnp.asarray(haar_table(), jnp.float32)
    forward_tables = dft_tables(-1.0)
    inverse_tables = dft_tables(1.0)
    target_device = dest_owner[:, 0]
    member = (target_device[:, None] == jnp.arange(vis_count, dtype=jnp.int32)[None, :]).astype(
        jnp.int32
    )
    earlier = jnp.cumsum(member, axis=0) - member
    position = target_device * capacity + jnp.sum(earlier * member, axis=1)
    slot_ids = (
        jnp.zeros((slot_total, 1), jnp.bfloat16)
        .at[position]
        .set(patch_slot[:, None].astype(jnp.bfloat16))
    )
    pack_v = jnp.zeros((slot_total,) + kernel_v.shape[1:], jnp.bfloat16).at[position].set(kernel_v)
    pack_u = jnp.zeros((slot_total,) + kernel_u.shape[1:], jnp.bfloat16).at[position].set(kernel_u)
    packed_measurements = (
        jnp.zeros((slot_total,) + measured.shape[1:], jnp.bfloat16).at[position].set(measured)
    )
    received_v_coords, received_u_coords, received_measurements, received_ids = (
        lax.all_to_all(pack_v, "vis", split_axis=0, concat_axis=0, tiled=True),
        lax.all_to_all(pack_u, "vis", split_axis=0, concat_axis=0, tiled=True),
        lax.all_to_all(packed_measurements, "vis", split_axis=0, concat_axis=0, tiled=True),
        lax.all_to_all(slot_ids, "vis", split_axis=0, concat_axis=0, tiled=True),
    )
    owning_device_ids = received_ids[:, 0].astype(jnp.int32)
    misfit = None
    estimate = image
    wav_index = lax.axis_index("wav")
    real_part, imag_part = dft_last(
        lax.all_to_all(estimate, "wav", split_axis=0, concat_axis=1, tiled=True),
        None,
        forward_tables,
        True,
    )
    stacked = jnp.stack([real_part, imag_part], 0)
    moved = lax.all_to_all(
        lax.all_to_all(stacked, "vis", split_axis=2, concat_axis=1, tiled=True),
        "wav",
        split_axis=2,
        concat_axis=1,
        tiled=True,
    )
    moved = (
        moved.reshape(2, wav_count, vis_count, strip, strip)
        .transpose(0, 4, 2, 1, 3)
        .reshape(2, strip, IMG)
    )
    real_part, imag_part = dft_last(moved[0], moved[1], forward_tables, True)
    blocks = (
        lax.all_to_all(
            jnp.stack([real_part, imag_part], 0).astype(jnp.bfloat16),
            "wav",
            split_axis=2,
            concat_axis=1,
            tiled=True,
        )
        .astype(jnp.float32)
        .reshape(2, tile_down, PATCH, tile_across, PATCH)
        .transpose(1, 3, 2, 0, 4)
    )
    misfit = degrid_values(
        received_v_coords,
        received_u_coords,
        blocks.reshape(patch_count, PATCH, 2 * PATCH).astype(jnp.bfloat16)[owning_device_ids],
        received_measurements,
    )
    onehot = (
        owning_device_ids[:, None] == jnp.arange(patch_count, dtype=jnp.int32)[None, :]
    ).astype(jnp.float32)
    summed = jnp.einsum(
        "sq,sac->qac",
        onehot,
        grid_terms(received_v_coords, received_u_coords, misfit),
        precision=HIGHEST,
    )
    blocks = summed.reshape(tile_down, tile_across, PATCH, 2, PATCH).transpose(3, 0, 2, 1, 4)
    grid_grad = blocks.reshape(2, kv_size, ku_size)
    moved = lax.all_to_all(
        grid_grad.astype(jnp.bfloat16), "wav", split_axis=1, concat_axis=2, tiled=True
    ).astype(grid_grad.dtype)
    real_part, imag_part = dft_last(moved[0], moved[1], inverse_tables, True)
    stacked = jnp.stack([real_part, imag_part], 0).transpose(0, 2, 1)
    moved = lax.all_to_all(
        lax.all_to_all(
            stacked.astype(jnp.bfloat16), "vis", split_axis=1, concat_axis=2, tiled=True
        ),
        "wav",
        split_axis=1,
        concat_axis=2,
        tiled=True,
    ).astype(stacked.dtype)
    moved = (
        moved.reshape(2, strip, wav_count, vis_count, strip)
        .transpose(0, 1, 3, 2, 4)
        .reshape(2, strip, IMG)
    )
    gradient = lax.all_to_all(
        dft_last(moved[0], moved[1], inverse_tables, False)[0].astype(jnp.bfloat16),
        "wav",
        split_axis=1,
        concat_axis=0,
        tiled=True,
    ).astype(jnp.float32)
    gathered = lax.all_gather(estimate - gradient, "wav", axis=1, tiled=True)
    single = basis_prox(gathered, wav_index, thresholds[wav_index], table)
    estimate = lax.psum_scatter(single, "wav", scatter_dimension=1, tiled=True) * (1.0 / wav_count)
    returned = lax.all_to_all(misfit, "vis", split_axis=0, concat_axis=0, tiled=True)
    residual = returned[position]
    return (estimate, residual)


def solution(mesh):
    in_specs = (
        P("vis", "wav"),
        P(("vis", "wav"), None, None),
        P(("vis", "wav"), None, None),
        P(("vis", "wav"), None, None),
        P(("vis", "wav"), None),
        P(("vis", "wav")),
        P(),
    )
    out_specs = (P("vis", "wav"), P(("vis", "wav"), None, None))
    return jax.shard_map(shards, mesh=mesh, in_specs=in_specs, out_specs=out_specs, check_vma=False)
```

profile of v0, /device:TPU:0, one launch (start us, length us, event | category | flops | bytes accessed | tf_op | source)
XLA Modules:
  0.0 1095.0 jit_solution(5774231187537844015)
XLA Ops:
  7.2 6.4 all-to-all-start.2
  14.0 47.7 %all-to-all-done.2 = f32[4,128,1024]{2,1,0:T(8,128)S(1)} async-done(((f32[4,128,1024]{2,1,0:T(8,128)}), f32[4,128,1024]{2,1,0:T(8,128)S(1)}, u32[]{:S(2)}, u32[]{:S(2)}) %all-to-all-start.2) | async-done | bytes 2097184 | tf_op jit(solution)/shard_map/all_to_all | solution.py:151
  88.0 15.6 %copy.220 = f32[2,128,4096]{1,0,2:T(2,128)S(1)} copy(f32[2,128,4096]{1,2,0:T(8,128)S(1)} %pad_maximum_fusion.1) | data formatting | bytes 8388608 | tf_op jit(solution)/shard_map/stack | solution.py:156
  103.6 52.6 %all_to_all.146 = f32[2,128,4096]{1,0,2:T(2,128)S(1)} all-to-all(f32[2,128,4096]{1,0,2:T(2,128)S(1)} %copy.220), channel_id=1, replica_groups=mesh['vis'=8,'wav'=4] {'vis'}, dimensions={2} | all-to-all | bytes 8388608 | tf_op jit(solution)/shard_map/all_to_all | solution.py:158
  158.5 5.3 copy.222
  163.8 7.4 copy.223
  176.6 10.1 scatter_custom_fusion
  189.3 79.8 %all-to-all-done.4 = f32[2,1024,512]{1,0,2:T(2,128)} async-done(((f32[2,1024,512]{1,0,2:T(2,128)}), f32[2,1024,512]{1,0,2:T(2,128)}, u32[]{:S(2)}, u32[]{:S(2)}) %all-to-all-start.4) | async-done | bytes 4194336 | tf_op jit(solution)/shard_map/all_to_all | solution.py:157
  272.4 5.5 copy.224
  278.0 5.3 copy.225
  296.5 6.3 fusion.19
  324.3 18.1 %copy.240 = bf16[2,128,4096]{1,0,2:T(2,128)(2,1)} copy(bf16[2,128,4096]{1,2,0:T(8,128)(2,1)S(1)} %pad_maximum_fusion.2) | data formatting | bytes 4194304 | tf_op jit(solution)/shard_map/stack | solution.py:172
  351.0 44.9 %all-to-all-done.5 = bf16[2,128,4096]{1,0,2:T(2,128)(2,1)} async-done(((bf16[2,128,4096]{1,0,2:T(2,128)(2,1)}), bf16[2,128,4096]{1,0,2:T(2,128)(2,1)}, u32[]{:S(2)}, u32[]{:S(2)}) %all-to-all-start.5) | async-done | bytes 2097184 | tf_op jit(solution)/shard_map/all_to_all | solution.py:171
  405.0 6.2 copy.241
  411.2 6.4 convert_element_type.212
  417.5 8.5 copy.242
  426.1 7.8 convert_element_type.214
  436.2 6.1 fusion.334
  470.3 5.5 convert_element_type.222
  483.1 48.8 %all-to-all-done.8 = bf16[2,512,1024]{2,0,1:T(2,128)(2,1)S(1)} async-done(((bf16[2,512,1024]{2,0,1:T(2,128)(2,1)}), bf16[2,512,1024]{2,0,1:T(2,128)(2,1)S(1)}, u32[]{:S(2)}, u32[]{:S(2)}) %all-to-all-start.8) | async-done | bytes 2097184 | tf_op jit(solution)/shard_map/all_to_all | solution.py:199
  559.5 17.8 %copy.260 = bf16[2,4096,128]{2,0,1:T(2,128)(2,1)S(1)} copy(bf16[2,4096,128]{2,1,0:T(8,128)(2,1)S(1)} %maximum_bitcast_fusion) | data formatting | bytes 4194304 | tf_op jit(solution)/shard_map/convert_element_type | solution.py:206
  577.3 30.2 %all_to_all.147 = bf16[2,4096,128]{2,0,1:T(2,128)(2,1)S(1)} all-to-all(bf16[2,4096,128]{2,0,1:T(2,128)(2,1)S(1)} %copy.260), channel_id=1, replica_groups=mesh['vis'=8,'wav'=4] {'vis'}, dimensions={1} | all-to-all | bytes 4194304 | tf_op jit(solution)/shard_map/all_to_all | solution.py:205
  615.4 50.4 %all_to_all.148 = bf16[2,512,1024]{2,0,1:T(2,128)(2,1)S(1)} all-to-all(bf16[2,512,1024]{2,0,1:T(2,128)(2,1)S(1)} %copy.263), channel_id=1, replica_groups=mesh['vis'=8,'wav'=4] {'wav'}, dimensions={1} | all-to-all | bytes 4194304 | tf_op jit(solution)/shard_map/all_to_all | solution.py:204
  686.1 27.8 %all_to_all.149 = bf16[128,4,1024]{0,2,1:T(8,128)(2,1)S(1)} all-to-all(bf16[128,4,1024]{0,2,1:T(8,128)(2,1)S(1)} %bitcast.254), channel_id=1, replica_groups=mesh['vis'=8,'wav'=4] {'wav'}, dimensions={1} | all-to-all | bytes 2097152 | tf_op jit(solution)/shard_map/all_to_all | solution.py:218
  723.6 145.7 %all-gather.2.cloned.1.call-done = f32[512,4096]{1,0:T(8,128)} async-done(((f32[512,1024]{1,0:T(8,128)}), f32[512,4096]{1,0:T(8,128)}) %all-gather.2.cloned.1.call-update) | async-done | bytes 8388624 | tf_op jit(solution)/shard_map/all_gather | solution.py:225
  869.3 11.0 %fusion.2 = f32[64,8,32,128]{3,1,2,0:T(8,128)} fusion(s32[]{:T(128)S(6)} %select_n.151, f32[512,4096]{1,0:T(8,128)} %all-gather.2.cloned.1.call-done), kind=kLoop, calls=%fused_computation.12 | loop fusion | flops 2097152 | bytes 16777220
  885.6 13.3 %fusion.5 = f32[256,2,32,128]{3,0,2,1:T(8,128)S(1)} fusion(f32[128,128,1,1]{1,0,3,2:T(8,128)S(1)} %copy-done.9, f32[256,2,32,128]{3,2,1,0:T(8,128)S(1)} %bitcast.221), kind=kOutput, calls=%fused_computation.16 | convolution fusion | flops 3221225472 | bytes 16842752 | tf_op jit(solution)/shard_map/rgj,kj->rgk/dot_general | solution.py:34
  907.7 13.4 %fusion.3 = f32[512,32,128]{0,2,1:T(8,128)} fusion(f32[128,128,1]{1,0,2:T(8,128)S(1)} %copy-done.8, f32[512,32,128]{2,1,0:T(8,128)S(1)} %bitcast.222), kind=kOutput, calls=%fused_computation.14 | convolution fusion | flops 3221225472 | bytes 16842752 | tf_op jit(solution)/shard_map/rgk,kj->rgj/dot_general | solution.py:43
  921.1 9.2 copy.280
  930.3 11.0 %fusion = f32[512,4096]{1,0:T(8,128)} fusion(s32[]{:T(128)S(6)} %select_n.153, f32[512,4096]{1,0:T(8,128)} %copy.280), kind=kLoop, calls=%fused_computation.10 | loop fusion | flops 2097152 | bytes 16777220 | tf_op jit(solution)/shard_map/jit(_roll_dynamic)/concatenate | solution.py:44
  945.1 5.5 all-to-all-done.12
  951.8 132.6 %reduce-scatter.2.cloned.1.call-done = f32[512,1024]{1,0:T(8,128)} async-done(((f32[512,4096]{1,0:T(8,128)}), f32[512,1024]{1,0:T(8,128)}) %reduce-scatter.2.cloned.1.call-update) | async-done | bytes 2097168 | tf_op jit(solution)/shard_map/reduce_scatter | solution.py:227
  (146 shorter events, 216.5 us)
Async XLA Ops:
  7.2 54.6 %all-to-all-start.2 = ((f32[4,128,1024]{2,1,0:T(8,128)}), f32[4,128,1024]{2,1,0:T(8,128)S(1)}, u32[]{:S(2)}, u32[]{:S(2)}) async-start(f32[4,128,1024]{2,1,0:T(8,128)} %bitcast.244), calls=%async_computation.2 | async-start | bytes 4194304 | tf_op jit(solution)/shard_map/all_to_all | solution.py:151
  61.7 1.3 copy-start.4
  171.2 5.0 copy-start.12
  171.2 5.0 copy-start.11
  171.2 97.9 %all-to-all-start.4 = ((f32[2,1024,512]{1,0,2:T(2,128)}), f32[2,1024,512]{1,0,2:T(2,128)}, u32[]{:S(2)}, u32[]{:S(2)}) async-start(f32[2,1024,512]{1,0,2:T(2,128)} %copy.223), calls=%async_computation.4 | async-start | bytes 8388608 | tf_op jit(solution)/shard_map/all_to_all | solution.py:157
  176.2 11.4 %copy-start.6 = (bf16[32,64,256]{2,1,0:T(8,128)(2,1)S(1)}, bf16[32,64,256]{2,1,0:T(8,128)(2,1)}, u32[]{:S(2)}) copy-start(bf16[32,64,256]{2,1,0:T(8,128)(2,1)} %param.11) | copy-start | bytes 3145732
  189.3 88.7 %copy-start.1 = (bf16[64,64,256]{2,1,0:T(8,128)(2,1)}, bf16[64,64,256]{2,1,0:T(8,128)(2,1)S(1)}, u32[]{:S(2)}) copy-start(bf16[64,64,256]{2,1,0:T(8,128)(2,1)S(1)} %scatter_fusion) | copy-start | bytes 6291460
  269.1 33.6 %all-to-all-start = ((bf16[8,8,1]{1,2,0:T(2,128)(2,1)}), bf16[8,8,1]{1,2,0:T(2,128)(2,1)S(1)}, u32[]{:S(2)}, u32[]{:S(2)}) async-start(bf16[8,8,1]{1,2,0:T(2,128)(2,1)} %all_to_all.132), calls=%async_computation | async-start | bytes 8192 | tf_op jit(solution)/shard_map/all_to_all | solution.py:144
  302.7 39.6 %all-to-all-start.1 = ((bf16[64,64,256]{2,1,0:T(8,128)(2,1)}), bf16[64,64,256]{2,1,0:T(8,128)(2,1)}, u32[]{:S(2)}, u32[]{:S(2)}) async-start(bf16[64,64,256]{2,1,0:T(8,128)(2,1)} %copy-done.1), calls=%async_computation.1 | async-start | bytes 4194304 | tf_op jit(solution)/shard_map/all_to_all | solution.py:141
  315.0 1.6 copy-start
  342.4 53.5 %all-to-all-start.5 = ((bf16[2,128,4096]{1,0,2:T(2,128)(2,1)}), bf16[2,128,4096]{1,0,2:T(2,128)(2,1)}, u32[]{:S(2)}, u32[]{:S(2)}) async-start(bf16[2,128,4096]{1,0,2:T(2,128)(2,1)} %copy.240), calls=%async_computation.5 | async-start | bytes 4194304 | tf_op jit(solution)/shard_map/all_to_all | solution.py:171
  346.9 1.2 copy-start.7
  349.7 1.3 copy-start.2
  351.0 49.6 %copy-start.10 = (bf16[32,2,256]{2,1,0:T(2,128)(2,1)S(1)}, bf16[32,2,256]{2,1,0:T(2,128)(2,1)}, u32[]{:S(2)}) copy-start(bf16[32,2,256]{2,1,0:T(2,128)(2,1)} %param.13) | copy-start | bytes 98308
  395.9 46.5 %all-to-all-start.6 = ((bf16[64,64,256]{2,1,0:T(8,128)(2,1)}), bf16[64,64,256]{2,1,0:T(8,128)(2,1)S(1)}, u32[]{:S(2)}, u32[]{:S(2)}) async-start(bf16[64,64,256]{2,1,0:T(8,128)(2,1)} %copy-done.2), calls=%async_computation.6 | async-start | bytes 4194304 | tf_op jit(solution)/shard_map/all_to_all | solution.py:142
  442.4 9.9 all-to-all-start.7
  479.2 52.7 %all-to-all-start.8 = ((bf16[2,512,1024]{2,0,1:T(2,128)(2,1)}), bf16[2,512,1024]{2,0,1:T(2,128)(2,1)S(1)}, u32[]{:S(2)}, u32[]{:S(2)}) async-start(bf16[2,512,1024]{2,0,1:T(2,128)(2,1)} %copy.245), calls=%async_computation.8 | async-start | bytes 4194304 | tf_op jit(solution)/shard_map/all_to_all | solution.py:199
  482.9 386.5 %all-gather.2.cloned.1.call-start = ((), (), s32[]{:S(2)}) async-start(), calls=%async_computation.14 | async-start | bytes 10485760 | tf_op jit(solution)/shard_map/all_gather | solution.py:225
  540.6 1.6 copy-start.5
  715.4 3.1 copy-start.3
  721.7 0.7 copy-start.13
  721.7 362.7 %reduce-scatter.2.cloned.1.call-start = ((), (), s32[]{:S(2)}) async-start(), calls=%async_computation.15 | async-start | bytes 10485760 | tf_op jit(solution)/shard_map/reduce_scatter | solution.py:227
  880.3 5.3 copy-start.9
  902.8 4.9 copy-start.8
  941.4 9.2 all-to-all-start.12
Sparse Core Ops, SparseCore 0:
  721.9 147.4 all-gather.1
  941.5 142.8 reduce-scatter.1
where the time goes:
time: 1110 us; the launch traced here: 1100 us
  waiting for transfers between devices  505 us (45%)
  local copies, waits for them, and re-layouts  205 us (18%)
  blocking collectives  161 us (15%)
  matrix products  126 us (11%)
  other arithmetic  42.6 us (4%)
  starting transfers between devices  39.5 us (4%)
  between operations  16 us (1%)
    all_gather x1, waiting for transfers between devices, shards(): gathered = lax.all_gather(estimate - gradient, 'wav', axis=1, tiled=True)  146 us
    reduce_scatter x1, waiting for transfers between devices, shards(): lax.psum_scatter(single, 'wav', scatter_dimension=1, tiled=True)  133 us
    all_to_all x1, waiting for transfers between devices, shards(): lax.all_to_all(lax.all_to_all(stacked, 'vis', split_axis=2, concat_axis=1...  79.8 us
    all_to_all x1, blocking collectives, shards(): lax.all_to_all(stacked, 'vis', split_axis=2, concat_axis=1, tiled=True)  52.6 us
    all_to_all x1, blocking collectives, shards(): lax.all_to_all(lax.all_to_all(stacked.astype(jnp.bfloat16), 'vis', split_...  50.4 us
    all_to_all x1, waiting for transfers between devices, shards(): lax.all_to_all(grid_grad.astype(jnp.bfloat16), 'wav', split_axis=1, conca...  48.8 us
    all_to_all x1, waiting for transfers between devices, shards(): lax.all_to_all(estimate, 'wav', split_axis=0, concat_axis=1, tiled=True)  47.7 us
    all_to_all x1, waiting for transfers between devices, shards(): lax.all_to_all(jnp.stack([real_part, imag_part], 0).astype(jnp.bfloat16),...  44.9 us
  transfers between devices with their start and end apart: 11, of which 7 were waited for; matrix products, arithmetic and copies ran while one was open for 12% of the time, Pallas kernels for 0%

commit v1 on v0

--- a/solution.py
+++ b/solution.py
@@ -10,6 +10,12 @@
 FA = 64
 FB = 64
 HIGHEST = lax.Precision.HIGHEST
+
+
+def joined_along(parts, dim):
+    parts = jnp.moveaxis(parts, 0, dim)
+    lengths = parts.shape
+    return parts.reshape(*lengths[:dim], lengths[dim] * lengths[dim + 1], *lengths[dim + 2 :])
 
 
 def haar_table():
@@ -222,7 +228,15 @@
         concat_axis=0,
         tiled=True,
     ).astype(jnp.float32)
-    gathered = lax.all_gather(estimate - gradient, "wav", axis=1, tiled=True)
+    x = estimate - gradient
+    size = lax.axis_size("wav")
+    right = [(i, (i + 1) % size) for i in range(size)]
+    tiles = [x]
+    while len(tiles) < size:
+        tiles.append(lax.ppermute(tiles[-1], "wav", right))
+    index_2 = lax.axis_index("wav")
+    tiles = jnp.stack(tiles)[(index_2 - jnp.arange(size)) % size]
+    gathered = joined_along(tiles, 1)
     single = basis_prox(gathered, wav_index, thresholds[wav_index], table)
     estimate = lax.psum_scatter(single, "wav", scatter_dimension=1, tiled=True) * (1.0 / wav_count)
     returned = lax.all_to_all(misfit, "vis", split_axis=0, concat_axis=0, tiled=True)

time: 1110 us -> 1130 us (1.018)
  local copies, waits for them, and re-layouts: 205 us -> 231 us
    all_gather x1 -> x0, waiting for transfers between devices: 146 us -> none  [shards(): gathered = lax.all_gather(estimate - gradient, 'wav', axis=1, tiled=True)]
    ppermute x0 -> x3, waiting for transfers between devices: none -> 140 us  [shards(): tiles.append(lax.ppermute(tiles[-1], 'wav', right))]
  transfers between devices with their start and end apart: 11 -> 13, of which waited for: 7 -> 9; matrix products, arithmetic and copies ran while one was open for 12% -> 12% of each run, Pallas kernels for 0% -> 0%
where the time goes in v1:
time: 1130 us; the launch traced here: 1120 us
  waiting for transfers between devices  498 us (44%)
  local copies, waits for them, and re-layouts  231 us (20%)
  blocking collectives  161 us (14%)
  matrix products  126 us (11%)
  other arithmetic  45.9 us (4%)
  starting transfers between devices  39.4 us (3%)
  between operations  16 us (1%)
    ppermute x3, waiting for transfers between devices, shards(): tiles.append(lax.ppermute(tiles[-1], 'wav', right))  140 us
    reduce_scatter x1, waiting for transfers between devices, shards(): lax.psum_scatter(single, 'wav', scatter_dimension=1, tiled=True)  132 us
    all_to_all x1, waiting for transfers between devices, shards(): lax.all_to_all(lax.all_to_all(stacked, 'vis', split_axis=2, concat_axis=1...  79.8 us
    all_to_all x1, blocking collectives, shards(): lax.all_to_all(stacked, 'vis', split_axis=2, concat_axis=1, tiled=True)  52.6 us
    all_to_all x1, blocking collectives, shards(): lax.all_to_all(lax.all_to_all(stacked.astype(jnp.bfloat16), 'vis', split_...  50.4 us
    all_to_all x1, waiting for transfers between devices, shards(): lax.all_to_all(grid_grad.astype(jnp.bfloat16), 'wav', split_axis=1, conca...  48.8 us
    all_to_all x1, waiting for transfers between devices, shards(): lax.all_to_all(estimate, 'wav', split_axis=0, concat_axis=1, tiled=True)  47.7 us
    all_to_all x1, waiting for transfers between devices, shards(): lax.all_to_all(jnp.stack([real_part, imag_part], 0).astype(jnp.bfloat16),...  44.9 us
  transfers between devices with their start and end apart: 13, of which 9 were waited for; matrix products, arithmetic and copies ran while one was open for 12% of the time, Pallas kernels for 0%

profile of v1, /device:TPU:0, one launch (start us, length us, event | category | flops | bytes accessed | tf_op | source)
XLA Modules:
  0.0 1117.6 jit_solution(16971265015000599979)
XLA Ops:
  7.2 6.4 all-to-all-start.2
  14.0 47.7 %all-to-all-done.2 = f32[4,128,1024]{2,1,0:T(8,128)S(1)} async-done(((f32[4,128,1024]{2,1,0:T(8,128)}), f32[4,128,1024]{2,1,0:T(8,128)S(1)}, u32[]{:S(2)}, u32[]{:S(2)}) %all-to-all-start.2) | async-done | bytes 2097184 | tf_op jit(solution)/shard_map/all_to_all | solution.py:157
  88.0 15.6 %copy.225 = f32[2,128,4096]{1,0,2:T(2,128)S(1)} copy(f32[2,128,4096]{1,2,0:T(8,128)S(1)} %pad_maximum_fusion.2) | data formatting | bytes 8388608 | tf_op jit(solution)/shard_map/stack | solution.py:162
  103.6 52.6 %all_to_all.146 = f32[2,128,4096]{1,0,2:T(2,128)S(1)} all-to-all(f32[2,128,4096]{1,0,2:T(2,128)S(1)} %copy.225), channel_id=1, replica_groups=mesh['vis'=8,'wav'=4] {'vis'}, dimensions={2} | all-to-all | bytes 8388608 | tf_op jit(solution)/shard_map/all_to_all | solution.py:164
  163.8 7.4 copy.228
  176.6 10.1 scatter_custom_fusion
  189.3 79.8 %all-to-all-done.4 = f32[2,1024,512]{1,0,2:T(2,128)} async-done(((f32[2,1024,512]{1,0,2:T(2,128)}), f32[2,1024,512]{1,0,2:T(2,128)}, u32[]{:S(2)}, u32[]{:S(2)}) %all-to-all-start.4) | async-done | bytes 4194336 | tf_op jit(solution)/shard_map/all_to_all | solution.py:163
  296.5 6.3 fusion.18
  324.3 18.1 %copy.245 = bf16[2,128,4096]{1,0,2:T(2,128)(2,1)} copy(bf16[2,128,4096]{1,2,0:T(8,128)(2,1)S(1)} %pad_maximum_fusion.3) | data formatting | bytes 4194304 | tf_op jit(solution)/shard_map/stack | solution.py:178
  351.1 44.9 %all-to-all-done.5 = bf16[2,128,4096]{1,0,2:T(2,128)(2,1)} async-done(((bf16[2,128,4096]{1,0,2:T(2,128)(2,1)}), bf16[2,128,4096]{1,0,2:T(2,128)(2,1)}, u32[]{:S(2)}, u32[]{:S(2)}) %all-to-all-start.5) | async-done | bytes 2097184 | tf_op jit(solution)/shard_map/all_to_all | solution.py:177
  405.1 6.2 copy.246
  411.3 6.3 convert_element_type.212
  417.6 8.6 copy.247
  426.2 7.8 convert_element_type.214
  436.3 6.2 fusion.335
  483.2 48.8 %all-to-all-done.8 = bf16[2,512,1024]{2,0,1:T(2,128)(2,1)S(1)} async-done(((bf16[2,512,1024]{2,0,1:T(2,128)(2,1)}), bf16[2,512,1024]{2,0,1:T(2,128)(2,1)S(1)}, u32[]{:S(2)}, u32[]{:S(2)}) %all-to-all-start.8) | async-done | bytes 2097184 | tf_op jit(solution)/shard_map/all_to_all | solution.py:205
  559.5 17.8 %copy.265 = bf16[2,4096,128]{2,0,1:T(2,128)(2,1)S(1)} copy(bf16[2,4096,128]{2,1,0:T(8,128)(2,1)S(1)} %maximum_bitcast_fusion) | data formatting | bytes 4194304 | tf_op jit(solution)/shard_map/convert_element_type | solution.py:212
  577.4 30.2 %all_to_all.147 = bf16[2,4096,128]{2,0,1:T(2,128)(2,1)S(1)} all-to-all(bf16[2,4096,128]{2,0,1:T(2,128)(2,1)S(1)} %copy.265), channel_id=1, replica_groups=mesh['vis'=8,'wav'=4] {'vis'}, dimensions={1} | all-to-all | bytes 4194304 | tf_op jit(solution)/shard_map/all_to_all | solution.py:211
  615.4 50.4 %all_to_all.148 = bf16[2,512,1024]{2,0,1:T(2,128)(2,1)S(1)} all-to-all(bf16[2,512,1024]{2,0,1:T(2,128)(2,1)S(1)} %copy.268), channel_id=1, replica_groups=mesh['vis'=8,'wav'=4] {'wav'}, dimensions={1} | all-to-all | bytes 4194304 | tf_op jit(solution)/shard_map/all_to_all | solution.py:210
  686.2 27.8 %all_to_all.149 = bf16[128,4,1024]{0,2,1:T(8,128)(2,1)S(1)} all-to-all(bf16[128,4,1024]{0,2,1:T(8,128)(2,1)S(1)} %bitcast.265), channel_id=1, replica_groups=mesh['vis'=8,'wav'=4] {'wav'}, dimensions={1} | all-to-all | bytes 2097152 | tf_op jit(solution)/shard_map/all_to_all | solution.py:224
  722.0 47.7 %collective-permute-done = f32[512,1024]{1,0:T(8,128)S(1)} collective-permute-done((f32[512,1024]{1,0:T(8,128)S(1)}, f32[512,1024]{1,0:T(8,128)S(1)}, u32[]{:S(2)}, u32[]{:S(2)}) %collective-permute-start) | collective-permute-done | bytes 2097184 | tf_op jit(solution)/shard_map/ppermute | solution.py:236
  769.7 47.1 %collective-permute-done.1 = f32[512,1024]{1,0:T(8,128)} collective-permute-done((f32[512,1024]{1,0:T(8,128)S(1)}, f32[512,1024]{1,0:T(8,128)}, u32[]{:S(2)}, u32[]{:S(2)}) %collective-permute-start.1) | collective-permute-done | bytes 2097184 | tf_op jit(solution)/shard_map/ppermute | solution.py:236
  818.1 45.2 %collective-permute-done.2 = f32[512,1024]{1,0:T(8,128)} collective-permute-done((f32[512,1024]{1,0:T(8,128)}, f32[512,1024]{1,0:T(8,128)}, u32[]{:S(2)}, u32[]{:S(2)}) %collective-permute-start.2) | collective-permute-done | bytes 2097184 | tf_op jit(solution)/shard_map/ppermute | solution.py:236
  869.0 7.7 gather_fusion.1
  876.7 8.8 copy.281
  885.5 9.9 fusion.1
  895.4 8.9 copy.282
  909.6 13.3 %fusion.4 = f32[256,2,32,128]{3,0,2,1:T(8,128)S(1)} fusion(f32[128,128,1,1]{1,0,3,2:T(8,128)S(1)} %copy-done.10, f32[256,2,32,128]{3,2,1,0:T(8,128)S(1)} %bitcast.228), kind=kOutput, calls=%fused_computation.17 | convolution fusion | flops 3221225472 | bytes 16842752 | tf_op jit(solution)/shard_map/rgj,kj->rgk/dot_general | solution.py:40
  931.7 13.4 %fusion.2 = f32[512,32,128]{0,2,1:T(8,128)} fusion(f32[128,128,1]{1,0,2:T(8,128)S(1)} %copy-done.9, f32[512,32,128]{2,1,0:T(8,128)S(1)} %bitcast.231), kind=kOutput, calls=%fused_computation.15 | convolution fusion | flops 3221225472 | bytes 16842752 | tf_op jit(solution)/shard_map/rgk,kj->rgj/dot_general | solution.py:49
  945.1 9.2 copy.287
  954.3 11.0 fusion
  975.4 131.6 %reduce-scatter.2.cloned.1.call-done = f32[512,1024]{1,0:T(8,128)} async-done(((f32[512,4096]{1,0:T(8,128)}), f32[512,1024]{1,0:T(8,128)}) %reduce-scatter.2.cloned.1.call-update) | async-done | bytes 2097168 | tf_op jit(solution)/shard_map/reduce_scatter | solution.py:241
  (157 shorter events, 248.7 us)
Async XLA Ops:
  7.2 54.6 %all-to-all-start.2 = ((f32[4,128,1024]{2,1,0:T(8,128)}), f32[4,128,1024]{2,1,0:T(8,128)S(1)}, u32[]{:S(2)}, u32[]{:S(2)}) async-start(f32[4,128,1024]{2,1,0:T(8,128)} %bitcast.254), calls=%async_computation.2 | async-start | bytes 4194304 | tf_op jit(solution)/shard_map/all_to_all | solution.py:157
  61.7 1.3 copy-start.4
  171.2 5.0 copy-start.13
  171.2 5.0 copy-start.12
  171.2 97.9 %all-to-all-start.4 = ((f32[2,1024,512]{1,0,2:T(2,128)}), f32[2,1024,512]{1,0,2:T(2,128)}, u32[]{:S(2)}, u32[]{:S(2)}) async-start(f32[2,1024,512]{1,0,2:T(2,128)} %copy.228), calls=%async_computation.4 | async-start | bytes 8388608 | tf_op jit(solution)/shard_map/all_to_all | solution.py:163
  176.2 11.4 %copy-start.7 = (bf16[32,64,256]{2,1,0:T(8,128)(2,1)S(1)}, bf16[32,64,256]{2,1,0:T(8,128)(2,1)}, u32[]{:S(2)}) copy-start(bf16[32,64,256]{2,1,0:T(8,128)(2,1)} %param.11) | copy-start | bytes 3145732
  189.3 88.7 %copy-start.1 = (bf16[64,64,256]{2,1,0:T(8,128)(2,1)}, bf16[64,64,256]{2,1,0:T(8,128)(2,1)S(1)}, u32[]{:S(2)}) copy-start(bf16[64,64,256]{2,1,0:T(8,128)(2,1)S(1)} %scatter_fusion) | copy-start | bytes 6291460
  269.1 33.6 %all-to-all-start = ((bf16[8,8,1]{1,2,0:T(2,128)(2,1)}), bf16[8,8,1]{1,2,0:T(2,128)(2,1)S(1)}, u32[]{:S(2)}, u32[]{:S(2)}) async-start(bf16[8,8,1]{1,2,0:T(2,128)(2,1)} %all_to_all.132), calls=%async_computation | async-start | bytes 8192 | tf_op jit(solution)/shard_map/all_to_all | solution.py:150
  302.8 39.6 %all-to-all-start.1 = ((bf16[64,64,256]{2,1,0:T(8,128)(2,1)}), bf16[64,64,256]{2,1,0:T(8,128)(2,1)}, u32[]{:S(2)}, u32[]{:S(2)}) async-start(bf16[64,64,256]{2,1,0:T(8,128)(2,1)} %copy-done.1), calls=%async_computation.1 | async-start | bytes 4194304 | tf_op jit(solution)/shard_map/all_to_all | solution.py:147
  315.1 1.6 copy-start
  342.4 53.5 %all-to-all-start.5 = ((bf16[2,128,4096]{1,0,2:T(2,128)(2,1)}), bf16[2,128,4096]{1,0,2:T(2,128)(2,1)}, u32[]{:S(2)}, u32[]{:S(2)}) async-start(bf16[2,128,4096]{1,0,2:T(2,128)(2,1)} %copy.245), calls=%async_computation.5 | async-start | bytes 4194304 | tf_op jit(solution)/shard_map/all_to_all | solution.py:177
  346.9 1.2 copy-start.8
  349.7 1.3 copy-start.2
  351.1 49.6 %copy-start.11 = (bf16[32,2,256]{2,1,0:T(2,128)(2,1)S(1)}, bf16[32,2,256]{2,1,0:T(2,128)(2,1)}, u32[]{:S(2)}) copy-start(bf16[32,2,256]{2,1,0:T(2,128)(2,1)} %param.13) | copy-start | bytes 98308
  396.0 46.5 %all-to-all-start.6 = ((bf16[64,64,256]{2,1,0:T(8,128)(2,1)}), bf16[64,64,256]{2,1,0:T(8,128)(2,1)S(1)}, u32[]{:S(2)}, u32[]{:S(2)}) async-start(bf16[64,64,256]{2,1,0:T(8,128)(2,1)} %copy-done.2), calls=%async_computation.6 | async-start | bytes 4194304 | tf_op jit(solution)/shard_map/all_to_all | solution.py:148
  442.4 9.9 all-to-all-start.7
  479.3 52.7 %all-to-all-start.8 = ((bf16[2,512,1024]{2,0,1:T(2,128)(2,1)}), bf16[2,512,1024]{2,0,1:T(2,128)(2,1)S(1)}, u32[]{:S(2)}, u32[]{:S(2)}) async-start(bf16[2,512,1024]{2,0,1:T(2,128)(2,1)} %copy.250), calls=%async_computation.8 | async-start | bytes 4194304 | tf_op jit(solution)/shard_map/all_to_all | solution.py:205
  482.9 624.1 %reduce-scatter.2.cloned.1.call-start = ((), (), s32[]{:S(2)}) async-start(), calls=%async_computation.14 | async-start | bytes 10485760 | tf_op jit(solution)/shard_map/reduce_scatter | solution.py:241
  540.6 1.6 copy-start.5
  715.4 3.0 copy-start.3
  718.5 98.4 %copy-start.14 = (f32[4]{0:T(128)S(1)}, f32[4]{0:T(128)}, u32[]{:S(2)}) copy-start(f32[4]{0:T(128)} %param.16) | copy-start | bytes 52
  720.5 1.3 copy-start.6
  721.8 47.9 %collective-permute-start = (f32[512,1024]{1,0:T(8,128)S(1)}, f32[512,1024]{1,0:T(8,128)S(1)}, u32[]{:S(2)}, u32[]{:S(2)}) collective-permute-start(f32[512,1024]{1,0:T(8,128)S(1)} %bitcast_subtract_fusion), channel_id=1, source_target_pairs={{0,1},{1,2},{2,3},{3,0},{4,5},{5,6},{6,7},{7,4},{8,9},{9,10},{10,1... | collective-permute-start | bytes 6291464 | tf_op jit(solution)/shard_map/ppermute | solution.py:236
  769.7 47.2 %collective-permute-start.1 = (f32[512,1024]{1,0:T(8,128)S(1)}, f32[512,1024]{1,0:T(8,128)}, u32[]{:S(2)}, u32[]{:S(2)}) collective-permute-start(f32[512,1024]{1,0:T(8,128)S(1)} %collective-permute-done), channel_id=1, source_target_pairs={{0,1},{1,2},{2,3},{3,0},{4,5},{5,6},{6,7},{7,4},{8,9},{9,10},{10,1... | collective-permute-start | bytes 6291464 | tf_op jit(solution)/shard_map/ppermute | solution.py:236
  816.9 46.5 %collective-permute-start.2 = (f32[512,1024]{1,0:T(8,128)}, f32[512,1024]{1,0:T(8,128)}, u32[]{:S(2)}, u32[]{:S(2)}) collective-permute-start(f32[512,1024]{1,0:T(8,128)} %collective-permute-done.1), channel_id=1, source_target_pairs={{0,1},{1,2},{2,3},{3,0},{4,5},{5,6},{6,7},{7,4},{8,9},{9,10},{10,1... | collective-permute-start | bytes 6291464 | tf_op jit(solution)/shard_map/ppermute | solution.py:236
  904.3 5.3 copy-start.10
  926.8 4.9 copy-start.9
  965.4 8.8 all-to-all-start.12
Sparse Core Ops, SparseCore 0:
  965.5 141.5 reduce-scatter.1
